TPU v7x, 32 devices: a whole 2x2x4 slice. The times are simulated.
32 devices in a mesh: batch: 4 (over x, core), hidden: 2 (over y), width: 4 (over z).
Axes of the slice: x: 2, y: 2, z: 4, core: 2. Of those that a mesh axis runs over, the one named last changes fastest.
Arguments:
- frames: bfloat16 [4, 512, 1280], P('batch', None, 'hidden'), may hold values from -6 to 6
- adapter_weight: bfloat16 [4, 1280, 16384], P(None, 'hidden', 'width'), may hold values from -0.078125 to 0.078125
- text_embed: bfloat16 [512, 16384], P('batch', 'width'), may hold values from -6 to 6
- audio_len: int32 [4], P('batch'), may hold values from 16 to 64, as said below
- text_len: int32 [4], P('batch'), may hold values from 32 to 112, as said below
- norm_gain: bfloat16 [16384], P('width'), may hold values from 0.5 to 1.5
- gate_up: bfloat16 [16384, 2, 26624], P('width', None, ('batch', 'hidden')), may hold values from -0.046875 to 0.046875
- cotangent: bfloat16 [512, 26624], P('width', ('batch', 'hidden')), may hold values from -0.59765625 to 0.59765625
Outputs:
- hidden: bfloat16 [512, 26624], P('width', ('batch', 'hidden'))
- weight_grad: float32 [4, 1280, 16384], P(None, 'hidden', 'width')
Inputs may be any that keep to these rules, and one draw needn't show every extreme that they name: `audio_len`: some sequence holds exactly 16 audio positions and another exactly 64. audio_len + text_len never exceeds 128, and equals it in some sequence.
All inputs are finite; a program needn't handle non-finite values.
Results may differ from a plain program's by a relative error of at most 0.0059.
Values may be sent and summed in bfloat16 or wider, within the bound.
No kernel may reach another device: no remote copies, remote signals or barrier semaphores. Data moves between devices by JAX's collectives and lax.ppermute only.
A program may use at most 256 MiB of HBM per device.

v0:
```python
import jax
import jax.numpy as jnp
from jax import lax
from jax.sharding import PartitionSpec as P

D = 16384
norm_eps = 1e-05


def row_lookup(table, row_index):
    slots = jnp.arange(table.shape[0], dtype=jnp.int32)
    return jnp.sum(jnp.where(row_index[:, None] == slots[None, :], table[None, :], 0), axis=1)


def on_device(
    frames, adapter_weight, text_embed, audio_len, text_len, norm_gain, gate_up, cotangent
):
    rows_here, frame_count, feat_here = frames.shape
    seq_len = frame_count // 4
    width_here = adapter_weight.shape[2]
    tok_here = rows_here * seq_len
    stacked = frames.reshape(tok_here, 4 * feat_here)
    kernel = adapter_weight.reshape(4 * feat_here, width_here)
    partial_audio = jnp.dot(stacked, kernel, preferred_element_type=jnp.float32)
    audio_part = lax.psum(partial_audio, "hidden")
    local_index = jnp.arange(tok_here, dtype=jnp.int32)
    row_index = local_index // seq_len
    positions = local_index % seq_len
    audio_count = row_lookup(audio_len, row_index)
    text_count = row_lookup(text_len, row_index)
    is_audio = positions < audio_count
    is_text = jnp.logical_and(jnp.logical_not(is_audio), positions < audio_count + text_count)
    stream = jnp.where(
        is_audio[:, None],
        audio_part,
        jnp.where(is_text[:, None], text_embed.astype(jnp.float32), jnp.zeros_like(audio_part)),
    )
    sum_squares = lax.psum(jnp.sum(stream * stream, axis=1), "width")
    inv_rms = lax.rsqrt(sum_squares / D + norm_eps)
    unit_stream = stream * inv_rms[:, None]
    gain_vals = norm_gain.astype(jnp.float32)
    normed = (unit_stream * gain_vals[None, :]).astype(jnp.bfloat16)
    weights = gate_up.reshape(width_here, -1)
    half_cols = weights.shape[1] // 2
    partial_pair = jnp.dot(
        lax.all_gather(normed, "batch", axis=0, tiled=True),
        weights,
        preferred_element_type=jnp.float32,
    )
    summed = lax.psum_scatter(partial_pair, "width", scatter_dimension=0, tiled=True)
    gate_vals = summed[:, :half_cols]
    up_vals = summed[:, half_cols:]
    sigmoid_gate = jax.nn.sigmoid(gate_vals)
    silu_gate = gate_vals * sigmoid_gate
    hidden = (silu_gate * up_vals).astype(jnp.bfloat16)
    cot_vals = cotangent.astype(jnp.float32)
    silu_slope = sigmoid_gate * (1.0 + gate_vals * (1.0 - sigmoid_gate))
    grad_pair = jnp.concatenate(
        [
            (cot_vals * up_vals * silu_slope).astype(jnp.bfloat16),
            (cot_vals * silu_gate).astype(jnp.bfloat16),
        ],
        axis=1,
    )
    all_pairs = lax.all_gather(grad_pair, "width", axis=0, tiled=True)
    share_rows = tok_here // lax.axis_size("hidden")
    row_block = all_pairs
    normed_grad = lax.psum_scatter(
        lax.dot_general(
            row_block, weights, (((1,), (1,)), ((), ())), preferred_element_type=jnp.float32
        ),
        ("batch", "hidden"),
        scatter_dimension=0,
        tiled=True,
    )
    share_start = lax.axis_index("hidden") * share_rows
    unit_share = lax.dynamic_slice_in_dim(unit_stream, share_start, share_rows, 0)
    inv_share = lax.dynamic_slice_in_dim(inv_rms, share_start, share_rows, 0)
    audio_share = lax.dynamic_slice_in_dim(is_audio, share_start, share_rows, 0)
    scaled_grad = normed_grad * gain_vals[None, :]
    proj_stat = lax.psum(jnp.sum(unit_share * scaled_grad, axis=1), "width") / D
    stream_grad = (scaled_grad - unit_share * proj_stat[:, None]) * inv_share[:, None]
    audio_grad = jnp.where(audio_share[:, None], stream_grad, jnp.zeros_like(stream_grad)).astype(
        jnp.bfloat16
    )
    all_frames = lax.all_gather(frames, "batch", axis=0, tiled=True)
    all_stacked = all_frames.reshape(-1, 4 * feat_here)
    row_block = all_stacked
    weight_grad = lax.dot_general(
        row_block,
        lax.all_gather(audio_grad, ("batch", "hidden"), axis=0, tiled=True),
        (((0,), (0,)), ((), ())),
        preferred_element_type=jnp.float32,
    )
    return (hidden, weight_grad.reshape(4, feat_here, width_here))


def solution(mesh):
    return jax.shard_map(
        on_device,
        mesh=mesh,
        in_specs=(
            P("batch", None, "hidden"),
            P(None, "hidden", "width"),
            P("batch", "width"),
            P("batch"),
            P("batch"),
            P("width"),
            P("width", None, ("batch", "hidden")),
            P("width", ("batch", "hidden")),
        ),
        out_specs=(P("width", ("batch", "hidden")), P(None, "hidden", "width")),
        check_vma=False,
    )
```

profile of v0, /device:TPU:0, one launch (start us, length us, event | category | flops | bytes accessed | tf_op | source)
XLA Modules:
  0.0 737.0 jit_solution(10051445883625385876)
XLA Ops:
  7.2 0.0 all-reduce.2.cloned.1.call-start
  7.2 1.5 reshape.67
  8.7 11.2 %fusion.8 = f32[128,4096]{1,0:T(8,128)} fusion(bf16[128,2560]{1,0:T(8,128)(2,1)S(1)} %reshape.67, bf16[2560,4096]{1,0:T(8,128)(2,1)} %bitcast.21), kind=kOutput, calls=%fused_computation.27 | convolution fusion | flops 2684354560 | bytes 23724032 | tf_op jit(solution)/shard_map/dot_general | solution.py:24
  19.9 0.0 copy-start.3
  19.9 0.0 copy-start.1
  19.9 0.0 all-reduce.2.cloned.1.call-update
  19.9 0.0 all-gather.5.cloned.1.call-start
  21.3 0.0 copy-done.3
  21.4 64.4 %all-reduce.2.cloned.1.call-done = f32[128,4096]{1,0:T(8,128)} async-done(((f32[128,4096]{1,0:T(8,128)}), f32[128,4096]{1,0:T(8,128)}) %all-reduce.2.cloned.1.call-update) | async-done | bytes 2097168 | tf_op jit(solution)/shard_map/psum | solution.py:25
  85.8 0.0 copy-done.1
  85.8 2.1 multiply_reduce_fusion
  87.9 11.7 %psum.22 = f32[128]{0:T(128)S(1)} all-reduce(f32[128]{0:T(128)S(1)} %multiply_reduce_fusion), channel_id=1, replica_groups=mesh['batch'=4,'hidden'=2,'width'=4] {'width'}, use_global_device_ids=true, to_apply=%region_2.3 | all-reduce | flops 128 | bytes 1024 | tf_op jit(solution)/shard_map/psum | solution.py:38
  99.6 3.2 multiply_convert_fusion
  102.7 0.0 all-gather.5.cloned.1.call-update
  102.8 0.0 reduce-scatter.3.cloned.1.call-start
  102.8 37.4 %copy.10 = bf16[512,8,2,3328]{3,1,2,0:T(8,128)(2,1)} copy(bf16[512,8,2,3328]{3,2,1,0:T(2,128)(2,1)} %bitcast.18) | data formatting | bytes 109051904
  140.2 0.0 all-gather.5.cloned.1.call-done
  140.2 38.9 %fusion.9 = f32[512,6656]{1,0:T(8,128)} fusion(bf16[512,4096]{1,0:T(8,128)(2,1)} %all-gather.5.cloned.1.call-done, bf16[4096,6656]{1,0:T(8,128)(2,1)} %bitcast.19), kind=kOutput, calls=%fused_computation.28 | convolution fusion | flops 27917287424 | bytes 72351744 | tf_op jit(solution)/shard_map/dot_general | solution.py:45
  179.1 0.0 copy-start.2
  179.1 0.0 reduce-scatter.3.cloned.1.call-update
  179.1 0.2 all-gather.7.cloned.1.call-start
  179.4 226.3 %reduce-scatter.3.cloned.1.call-done = f32[128,6656]{1,0:T(8,128)} async-done(((f32[512,6656]{1,0:T(8,128)}), f32[128,6656]{1,0:T(8,128)}) %reduce-scatter.3.cloned.1.call-update) | async-done | bytes 3407888 | tf_op jit(solution)/shard_map/reduce_scatter | solution.py:50
  405.7 0.0 copy-done.2
  405.7 3.9 fusion.1
  409.5 1.3 pad_maximum_fusion
  410.8 0.0 all-gather.7.cloned.1.call-update
  410.9 0.0 reduce-scatter.5.cloned.1.call-start
  410.9 125.0 %all-gather.7.cloned.1.call-done = bf16[512,6656]{1,0:T(8,128)(2,1)} async-done(((bf16[128,6656]{1,0:T(8,128)(2,1)}), bf16[512,6656]{1,0:T(8,128)(2,1)}) %all-gather.7.cloned.1.call-update) | async-done | bytes 6815760 | tf_op jit(solution)/shard_map/all_gather | solution.py:65
  536.0 35.6 %fusion.10 = f32[512,4096]{1,0:T(8,128)} fusion(bf16[512,6656]{1,0:T(8,128)(2,1)} %all-gather.7.cloned.1.call-done, bf16[4096,6656]{1,0:T(8,128)(2,1)} %bitcast.20), kind=kOutput, calls=%fused_computation.29 | convolution fusion | flops 27917287424 | bytes 69730304 | tf_op jit(solution)/shard_map/dot_general | solution.py:69
  571.5 0.0 reduce-scatter.5.cloned.1.call-update
  571.5 0.0 all-gather.11.cloned.1.call-start
  571.6 0.5 all-gather.11.cloned.1.call-update
  572.1 0.0 all-gather.9.cloned.1.call-start
  572.2 0.1 dynamic_slice.9
  572.3 0.1 dynamic_slice.11
  572.3 69.1 %reduce-scatter.5.cloned.1.call-done = f32[64,4096]{1,0:T(8,128)} async-done(((f32[512,4096]{1,0:T(8,128)}), f32[64,4096]{1,0:T(8,128)}) %reduce-scatter.5.cloned.1.call-update) | async-done | bytes 1048592 | tf_op jit(solution)/shard_map/reduce_scatter | solution.py:68
  641.4 0.0 copy-start
  641.4 1.5 multiply_reduce_fusion.1
  642.9 11.7 %psum.23 = f32[64]{0:T(128)S(1)} all-reduce(f32[64]{0:T(128)S(1)} %multiply_reduce_fusion.1), channel_id=1, replica_groups=mesh['batch'=4,'hidden'=2,'width'=4] {'width'}, use_global_device_ids=true, to_apply=%region_6.7 | all-reduce | flops 64 | bytes 512 | tf_op jit(solution)/shard_map/psum | solution.py:81
  654.6 0.0 copy-done
  654.6 1.0 select_convert_fusion
  655.7 0.0 all-gather.9.cloned.1.call-update
  655.7 12.7 %all-gather.11.cloned.1.call-done = bf16[4,512,640]{2,1,0:T(8,128)(2,1)} async-done(((bf16[1,512,640]{2,1,0:T(8,128)(2,1)}), bf16[4,512,640]{2,1,0:T(8,128)(2,1)}) %all-gather.11.cloned.1.call-update) | async-done | bytes 2621456 | tf_op jit(solution)/shard_map/all_gather | solution.py:86
  668.4 5.3 reshape.70
  673.7 33.7 %all-gather.9.cloned.1.call-done = bf16[512,4096]{1,0:T(8,128)(2,1)} async-done(((bf16[64,4096]{1,0:T(8,128)(2,1)}), bf16[512,4096]{1,0:T(8,128)(2,1)}) %all-gather.9.cloned.1.call-update) | async-done | bytes 4194320 | tf_op jit(solution)/shard_map/all_gather | solution.py:91
  707.4 22.7 %fusion.11 = f32[4096,2560]{0,1:T(8,128)} fusion(bf16[512,4096]{1,0:T(8,128)(2,1)} %all-gather.9.cloned.1.call-done, bf16[512,2560]{1,0:T(8,128)(2,1)} %reshape.70), kind=kOutput, calls=%fused_computation.30 | convolution fusion | flops 10737418240 | bytes 48758784 | tf_op jit(solution)/shard_map/dot_general | solution.py:89
  (4 shorter events, 0.0 us)
Async XLA Ops:
  7.2 78.6 %all-reduce.2.cloned.1.call-start = ((), (), s32[]{:S(2)}) async-start(), calls=%async_computation.2 | async-start | bytes 4194304 | tf_op jit(solution)/shard_map/psum | solution.py:25
  19.9 1.5 copy-start.3
  19.9 65.9 %copy-start.1 = (bf16[128,4096]{1,0:T(8,128)(2,1)S(1)}, bf16[128,4096]{1,0:T(8,128)(2,1)}, u32[]{:S(2)}) copy-start(bf16[128,4096]{1,0:T(8,128)(2,1)} %param.10) | copy-start | bytes 3145732
  19.9 120.3 %all-gather.5.cloned.1.call-start = ((), (), s32[]{:S(2)}) async-start(), calls=%async_computation.3 | async-start | bytes 5242880 | tf_op jit(solution)/shard_map/all_gather | solution.py:46
  102.8 302.9 %reduce-scatter.3.cloned.1.call-start = ((), (), s32[]{:S(2)}) async-start(), calls=%async_computation.4 | async-start | bytes 17039360 | tf_op jit(solution)/shard_map/reduce_scatter | solution.py:50
  179.1 226.6 %copy-start.2 = (bf16[128,3328]{1,0:T(8,128)(2,1)S(1)}, bf16[128,3328]{1,0:T(8,128)(2,1)}, u32[]{:S(2)}) copy-start(bf16[128,3328]{1,0:T(8,128)(2,1)} %param.15) | copy-start | bytes 2555908
  179.1 356.8 %all-gather.7.cloned.1.call-start = ((), (), s32[]{:S(2)}) async-start(), calls=%async_computation.5 | async-start | bytes 8519680 | tf_op jit(solution)/shard_map/all_gather | solution.py:65
  410.9 230.5 %reduce-scatter.5.cloned.1.call-start = ((), (), s32[]{:S(2)}) async-start(), calls=%async_computation.6 | async-start | bytes 9437184 | tf_op jit(solution)/shard_map/reduce_scatter | solution.py:68
  571.5 96.8 %all-gather.11.cloned.1.call-start = ((), (), s32[]{:S(2)}) async-start(), calls=%async_computation.8 | async-start | bytes 3276800 | tf_op jit(solution)/shard_map/all_gather | solution.py:86
  572.1 135.3 %all-gather.9.cloned.1.call-start = ((), (), s32[]{:S(2)}) async-start(), calls=%async_computation.7 | async-start | bytes 4718592 | tf_op jit(solution)/shard_map/all_gather | solution.py:91
  641.4 13.2 %copy-start = (f32[64,4096]{1,0:T(8,128)S(1)}, f32[64,4096]{1,0:T(8,128)}, u32[]{:S(2)}) copy-start(f32[64,4096]{1,0:T(8,128)} %reduce-scatter.5.cloned.1.call-done) | copy-start | bytes 3145732
Sparse Core Ops, SparseCore 0:
  20.0 65.6 all-reduce.1
  102.9 31.6 all-gather.4
  179.3 226.3 reduce-scatter.2
  411.0 124.9 all-gather.6
  571.7 69.6 reduce-scatter.4
  642.8 25.5 all-gather.10
  670.8 36.5 all-gather.8
where the time goes:
time: 737 us
  waiting for transfers between devices  532 us (72%)
  matrix products  108 us (15%)
  local copies, waits for them, and re-layouts  44.4 us (6%)
  blocking collectives  23.4 us (3%)
  between operations  15.5 us (2%)
  other arithmetic  13 us (2%)
    reduce_scatter x1, waiting for transfers between devices, on_device(): lax.psum_scatter(partial_pair, 'width', scatter_dimension=0, tiled=True)  226 us
    all_gather x1, waiting for transfers between devices, on_device(): all_pairs = lax.all_gather(grad_pair, 'width', axis=0, tiled=True)  125 us
    reduce_scatter x1, waiting for transfers between devices, on_device(): lax.psum_scatter(lax.dot_general(row_block, weights, (((1,), (1,)), ((),...  69.1 us
    psum x1, waiting for transfers between devices, on_device(): audio_part = lax.psum(partial_audio, 'hidden')  64.4 us
    dot_general x1, matrix products, on_device(): jnp.dot(lax.all_gather(normed, 'batch', axis=0, tiled=True), weights, pre...  38.9 us
    unnamed x9, local copies, waits for them, and re-layouts  37.4 us
    dot_general x1, matrix products, on_device(): lax.dot_general(row_block, weights, (((1,), (1,)), ((), ())), preferred_e...  35.6 us
    all_gather x1, waiting for transfers between devices, on_device(): lax.all_gather(audio_grad, ('batch', 'hidden'), axis=0, tiled=True)  33.7 us
  transfers between devices with their start and end apart: 7, of which 6 were waited for; matrix products, arithmetic and copies ran while one was open for 6% of the time, Pallas kernels for 0%

commit v1 on v0

--- a/solution.py
+++ b/solution.py
@@ -22,7 +22,7 @@
     stacked = frames.reshape(tok_here, 4 * feat_here)
     kernel = adapter_weight.reshape(4 * feat_here, width_here)
     partial_audio = jnp.dot(stacked, kernel, preferred_element_type=jnp.float32)
-    audio_part = lax.psum(partial_audio, "hidden")
+    audio_part = jnp.sum(lax.all_gather(partial_audio, "hidden"), axis=0)
     local_index = jnp.arange(tok_here, dtype=jnp.int32)
     row_index = local_index // seq_len
     positions = local_index % seq_len

time: 737 us -> 728 us (0.988)
    psum x1 -> x0, waiting for transfers between devices: 64.4 us -> none  [on_device(): audio_part = lax.psum(partial_audio, 'hidden')]
    all_gather x0 -> x1, waiting for transfers between devices: none -> 58.2 us  [on_device(): audio_part = jnp.sum(lax.all_gather(partial_audio, 'hidden'), axis=0)]
    unnamed x9 -> x11, local copies, waits for them, and re-layouts: 37.4 us -> 37.7 us
where the time goes in v1:
time: 728 us
  waiting for transfers between devices  526 us (72%)
  matrix products  105 us (14%)
  local copies, waits for them, and re-layouts  43.5 us (6%)
  blocking collectives  23.6 us (3%)
  between operations  15.5 us (2%)
  other arithmetic  13.3 us (2%)
    reduce_scatter x1, waiting for transfers between devices, on_device(): lax.psum_scatter(partial_pair, 'width', scatter_dimension=0, tiled=True)  226 us
    all_gather x1, waiting for transfers between devices, on_device(): all_pairs = lax.all_gather(grad_pair, 'width', axis=0, tiled=True)  125 us
    reduce_scatter x1, waiting for transfers between devices, on_device(): lax.psum_scatter(lax.dot_general(row_block, weights, (((1,), (1,)), ((),...  69 us
    all_gather x1, waiting for transfers between devices, on_device(): audio_part = jnp.sum(lax.all_gather(partial_audio, 'hidden'), axis=0)  58.2 us
    dot_general x1, matrix products, on_device(): jnp.dot(lax.all_gather(normed, 'batch', axis=0, tiled=True), weights, pre...  38.8 us
    unnamed x11, local copies, waits for them, and re-layouts  37.7 us
    dot_general x1, matrix products, on_device(): lax.dot_general(row_block, weights, (((1,), (1,)), ((), ())), preferred_e...  35.6 us
    all_gather x1, waiting for transfers between devices, on_device(): lax.all_gather(audio_grad, ('batch', 'hidden'), axis=0, tiled=True)  35 us
  transfers between devices with their start and end apart: 7, of which 6 were waited for; matrix products, arithmetic and copies ran while one was open for 6% of the time, Pallas kernels for 0%

profile of v1, /device:TPU:0, one launch (start us, length us, event | category | flops | bytes accessed | tf_op | source)
XLA Modules:
  0.0 728.0 jit_solution(12098308574365659535)
XLA Ops:
  7.2 0.0 all-gather.15.cloned.1.call-start
  7.2 1.5 reshape.67
  8.7 11.2 %fusion.8 = f32[128,4096]{1,0:T(8,128)} fusion(bf16[128,2560]{1,0:T(8,128)(2,1)S(1)} %reshape.67, bf16[2560,4096]{1,0:T(8,128)(2,1)} %bitcast.22), kind=kOutput, calls=%fused_computation.27 | convolution fusion | flops 2684354560 | bytes 23724032 | tf_op jit(solution)/shard_map/dot_general | solution.py:24
  19.9 0.0 copy-start.4
  19.9 0.0 all-gather.15.cloned.1.call-update
  19.9 0.0 all-gather.7.cloned.1.call-start
  21.3 0.0 copy-done.4
  21.3 58.2 %all-gather.15.cloned.1.call-done = f32[256,4096]{1,0:T(8,128)} async-done(((f32[128,4096]{1,0:T(8,128)}), f32[256,4096]{1,0:T(8,128)}) %all-gather.15.cloned.1.call-update) | async-done | bytes 4194320 | tf_op jit(solution)/shard_map/all_gather | solution.py:25
  79.5 0.0 copy-start.2
  79.5 2.8 reduce_sum.27
  82.3 0.0 copy-done.2
  82.3 0.5 multiply_reduce_fusion
  82.8 11.7 %psum.14 = f32[128]{0:T(128)S(1)} all-reduce(f32[128]{0:T(128)S(1)} %multiply_reduce_fusion), channel_id=1, replica_groups=mesh['batch'=4,'hidden'=2,'width'=4] {'width'}, use_global_device_ids=true, to_apply=%region_2.3 | all-reduce | flops 128 | bytes 1024 | tf_op jit(solution)/shard_map/psum | solution.py:38
  94.5 2.3 multiply_convert_fusion
  96.8 0.0 all-gather.7.cloned.1.call-update
  96.8 0.2 reduce-scatter.3.cloned.1.call-start
  97.0 37.7 %copy.10 = bf16[512,8,2,3328]{3,1,2,0:T(8,128)(2,1)} copy(bf16[512,8,2,3328]{3,2,1,0:T(2,128)(2,1)} %bitcast.19) | data formatting | bytes 109051904
  134.7 0.0 all-gather.7.cloned.1.call-done
  134.7 38.8 %fusion.9 = f32[512,6656]{1,0:T(8,128)} fusion(bf16[512,4096]{1,0:T(8,128)(2,1)} %all-gather.7.cloned.1.call-done, bf16[4096,6656]{1,0:T(8,128)(2,1)} %bitcast.20), kind=kOutput, calls=%fused_computation.28 | convolution fusion | flops 27917287424 | bytes 72351744 | tf_op jit(solution)/shard_map/dot_general | solution.py:45
  173.5 0.0 copy-start.3
  173.5 0.0 reduce-scatter.3.cloned.1.call-update
  173.5 0.0 all-gather.9.cloned.1.call-start
  173.6 226.0 %reduce-scatter.3.cloned.1.call-done = f32[128,6656]{1,0:T(8,128)} async-done(((f32[512,6656]{1,0:T(8,128)}), f32[128,6656]{1,0:T(8,128)}) %reduce-scatter.3.cloned.1.call-update) | async-done | bytes 3407888 | tf_op jit(solution)/shard_map/reduce_scatter | solution.py:50
  399.6 0.0 copy-done.3
  399.6 3.9 fusion.1
  403.5 1.3 pad_maximum_fusion
  404.8 0.0 all-gather.9.cloned.1.call-update
  404.8 0.0 reduce-scatter.5.cloned.1.call-start
  404.8 125.1 %all-gather.9.cloned.1.call-done = bf16[512,6656]{1,0:T(8,128)(2,1)} async-done(((bf16[128,6656]{1,0:T(8,128)(2,1)}), bf16[512,6656]{1,0:T(8,128)(2,1)}) %all-gather.9.cloned.1.call-update) | async-done | bytes 6815760 | tf_op jit(solution)/shard_map/all_gather | solution.py:65
  529.9 35.6 %fusion.10 = f32[512,4096]{1,0:T(8,128)} fusion(bf16[512,6656]{1,0:T(8,128)(2,1)} %all-gather.9.cloned.1.call-done, bf16[4096,6656]{1,0:T(8,128)(2,1)} %bitcast.21), kind=kOutput, calls=%fused_computation.29 | convolution fusion | flops 27917287424 | bytes 69730304 | tf_op jit(solution)/shard_map/dot_general | solution.py:69
  565.5 0.0 copy-start
  565.5 0.0 reduce-scatter.5.cloned.1.call-update
  565.5 0.0 all-gather.13.cloned.1.call-start
  565.6 0.5 all-gather.13.cloned.1.call-update
  566.1 0.0 all-gather.11.cloned.1.call-start
  566.1 0.1 dynamic_slice.9
  566.2 0.1 dynamic_slice.11
  566.3 69.0 %reduce-scatter.5.cloned.1.call-done = f32[64,4096]{1,0:T(8,128)} async-done(((f32[512,4096]{1,0:T(8,128)}), f32[64,4096]{1,0:T(8,128)}) %reduce-scatter.5.cloned.1.call-update) | async-done | bytes 1048592 | tf_op jit(solution)/shard_map/reduce_scatter | solution.py:68
  635.3 0.0 copy-done
  635.3 1.5 multiply_reduce_fusion.1
  636.9 11.9 %psum.15 = f32[64]{0:T(128)S(1)} all-reduce(f32[64]{0:T(128)S(1)} %multiply_reduce_fusion.1), channel_id=1, replica_groups=mesh['batch'=4,'hidden'=2,'width'=4] {'width'}, use_global_device_ids=true, to_apply=%region_6.7 | all-reduce | flops 64 | bytes 512 | tf_op jit(solution)/shard_map/psum | solution.py:81
  648.8 0.0 copy-done.1
  648.8 1.0 select_convert_fusion
  649.8 0.0 all-gather.11.cloned.1.call-update
  649.9 12.5 %all-gather.13.cloned.1.call-done = bf16[4,512,640]{2,1,0:T(8,128)(2,1)} async-done(((bf16[1,512,640]{2,1,0:T(8,128)(2,1)}), bf16[4,512,640]{2,1,0:T(8,128)(2,1)}) %all-gather.13.cloned.1.call-update) | async-done | bytes 2621456 | tf_op jit(solution)/shard_map/all_gather | solution.py:86
  662.3 4.1 reshape.70
  666.4 35.0 %all-gather.11.cloned.1.call-done = bf16[512,4096]{1,0:T(8,128)(2,1)} async-done(((bf16[64,4096]{1,0:T(8,128)(2,1)}), bf16[512,4096]{1,0:T(8,128)(2,1)}) %all-gather.11.cloned.1.call-update) | async-done | bytes 4194320 | tf_op jit(solution)/shard_map/all_gather | solution.py:91
  701.4 19.7 %fusion.11 = f32[4096,2560]{0,1:T(8,128)} fusion(bf16[512,4096]{1,0:T(8,128)(2,1)} %all-gather.11.cloned.1.call-done, bf16[512,2560]{1,0:T(8,128)(2,1)S(1)} %reshape.70), kind=kOutput, calls=%fused_computation.30 | convolution fusion | flops 10737418240 | bytes 48758784 | tf_op jit(solution)/shard_map/dot_general | solution.py:89
  (5 shorter events, 0.0 us)
Async XLA Ops:
  7.2 72.4 %all-gather.15.cloned.1.call-start = ((), (), s32[]{:S(2)}) async-start(), calls=%async_computation.8 | async-start | bytes 6291456 | tf_op jit(solution)/shard_map/all_gather | solution.py:25
  19.9 1.4 copy-start.4
  19.9 114.8 %all-gather.7.cloned.1.call-start = ((), (), s32[]{:S(2)}) async-start(), calls=%async_computation.2 | async-start | bytes 5242880 | tf_op jit(solution)/shard_map/all_gather | solution.py:46
  79.5 2.8 copy-start.2
  96.8 302.8 %reduce-scatter.3.cloned.1.call-start = ((), (), s32[]{:S(2)}) async-start(), calls=%async_computation.3 | async-start | bytes 17039360 | tf_op jit(solution)/shard_map/reduce_scatter | solution.py:50
  173.5 226.1 %copy-start.3 = (bf16[128,3328]{1,0:T(8,128)(2,1)S(1)}, bf16[128,3328]{1,0:T(8,128)(2,1)}, u32[]{:S(2)}) copy-start(bf16[128,3328]{1,0:T(8,128)(2,1)} %param.15) | copy-start | bytes 2555908
  173.5 356.4 %all-gather.9.cloned.1.call-start = ((), (), s32[]{:S(2)}) async-start(), calls=%async_computation.4 | async-start | bytes 8519680 | tf_op jit(solution)/shard_map/all_gather | solution.py:65
  404.8 230.5 %reduce-scatter.5.cloned.1.call-start = ((), (), s32[]{:S(2)}) async-start(), calls=%async_computation.5 | async-start | bytes 9437184 | tf_op jit(solution)/shard_map/reduce_scatter | solution.py:68
  565.5 69.9 %copy-start = (f32[128,4096]{1,0:T(8,128)S(1)}, f32[128,4096]{1,0:T(8,128)}, u32[]{:S(2)}) copy-start(f32[128,4096]{1,0:T(8,128)} %get-tuple-element.3) | copy-start | bytes 6291460
  565.5 96.8 %all-gather.13.cloned.1.call-start = ((), (), s32[]{:S(2)}) async-start(), calls=%async_computation.7 | async-start | bytes 3276800 | tf_op jit(solution)/shard_map/all_gather | solution.py:86
  566.1 135.3 %all-gather.11.cloned.1.call-start = ((), (), s32[]{:S(2)}) async-start(), calls=%async_computation.6 | async-start | bytes 4718592 | tf_op jit(solution)/shard_map/all_gather | solution.py:91
  635.3 13.5 %copy-start.1 = (f32[64,4096]{1,0:T(8,128)S(1)}, f32[64,4096]{1,0:T(8,128)}, u32[]{:S(2)}) copy-start(f32[64,4096]{1,0:T(8,128)} %reduce-scatter.5.cloned.1.call-done) | copy-start | bytes 3145732
Sparse Core Ops, SparseCore 0:
  20.0 59.4 all-gather.14
  96.9 31.6 all-gather.6
  173.7 225.9 reduce-scatter.2
  404.9 124.9 all-gather.8
  565.6 69.6 reduce-scatter.4
  636.7 25.5 all-gather.12
  664.8 36.5 all-gather.10
